TPU v7x, 256 devices: a whole 4x4x8 slice. The times are simulated.
256 devices in a mesh: tile: 4 (over y), proj: 16 (over x, z_hi, core), cuts: 4 (over z_lo).
Axes of the slice: x: 4, y: 4, z: 8 (z_hi: 2, z_lo: 4; z = z_hi * 4 + z_lo), core: 2. Of those that a mesh axis runs over, the one named last changes fastest.
Arguments:
- object_field: float32 [64, 2, 384, 2048], P(('proj', 'cuts'), None, None, 'tile'), may hold values from -5 to 5
- probe_field: float32 [2, 256, 256], replicated, may hold values from -6 to 6
- amplitudes: bfloat16 [64, 4, 6, 256, 256], P(('proj', 'cuts'), 'tile'), may hold values from 0 to 16
- pos_rows: int32 [64, 4, 6], P(('proj', 'cuts'), 'tile'), may hold values from 0 to 128
- pos_cols: int32 [64, 4, 6], P(('proj', 'cuts'), 'tile'), may hold values from 0 to 512
- counts: int32 [64, 4], P(('proj', 'cuts'), 'tile'), may hold values from 1 to 6, as said below
- admm_dual: float32 [64, 32, 2048], P(('proj', 'cuts'), None, 'tile'), may hold values from -4 to 4
- volume: float32 [32, 2048, 2048], P('cuts', ('tile', 'proj')), may hold values from -6 to 6
- proj_weights: bfloat16 [16, 2048, 2048], P(None, ('tile', 'proj')), may hold values from -0.125 to 0.125
- ray_weights: float32 [16, 2048], replicated, may hold values from -0.125 to 0.125
- angle_ids: int32 [64], replicated, may hold values from 0 to 15
Outputs:
- new_object: float32 [64, 2, 384, 2048], P(('proj', 'cuts'), None, None, 'tile')
- new_probe: float32 [2, 256, 256], replicated
- new_volume: float32 [32, 2048, 2048], P('cuts', ('tile', 'proj'))
Inputs may be any that keep to these rules, and one draw needn't show every extreme that they name: `counts`: every tile holds at least one live position and at most 6; exactly one tile of one projection holds 6, every other holds at most 3.
All inputs are finite; a program needn't handle non-finite values.
Results may differ from a plain program's by a relative error of at most 0.00095.
The roundings to bfloat16 on the way count: a program that leaves them out, or rounds other values in their place, can miss the bound.
Values may be sent and summed in bfloat16 or wider, within the bound.
A program may use at most 64 MiB of HBM per device.

v0:
```python
import math
import jax
import jax.numpy as jnp
from jax import lax
from jax.sharding import PartitionSpec as P

PB = 256
tomo_step = 1.0


def shifted(value, axis, steps):
    count = lax.axis_size(axis)
    leading, last = (max(0, -steps), min(count, count - steps))
    return lax.ppermute(value, axis, [(source, source + steps) for source in range(leading, last)])


def dft_tables(side):
    indices = jnp.arange(side, dtype=jnp.int32)
    products = indices[:, None] * indices[None, :] % side
    phase_angle = products.astype(jnp.float32) * (2.0 * math.pi / side)
    norm_factor = 1.0 / math.sqrt(side)
    return (
        (jnp.cos(phase_angle) * norm_factor).astype(jnp.bfloat16),
        (-jnp.sin(phase_angle) * norm_factor).astype(jnp.bfloat16),
    )


def matmul(left, right):
    return jnp.dot(left, right, preferred_element_type=jnp.float32)


def complex_matmul(left_real, left_imag, right_real, right_imag):
    out_real = matmul(left_real, right_real) - matmul(left_imag, right_imag)
    out_imag = matmul(left_real, right_imag) + matmul(left_imag, right_real)
    return (out_real, out_imag)


def patch_terms(patch_real, patch_imag, probe_real, probe_imag, amplitude, dft_real, dft_imag):
    wave_real = (probe_real * patch_real - probe_imag * patch_imag).astype(jnp.bfloat16)
    wave_imag = (probe_real * patch_imag + probe_imag * patch_real).astype(jnp.bfloat16)
    half_real, half_imag = complex_matmul(dft_real, dft_imag, wave_real, wave_imag)
    half_real = half_real.astype(jnp.bfloat16)
    half_imag = half_imag.astype(jnp.bfloat16)
    far_real, far_imag = complex_matmul(half_real, half_imag, dft_real, dft_imag)
    modulus = jnp.sqrt(far_real * far_real + far_imag * far_imag + 0.25)
    factor = amplitude.astype(jnp.float32) / modulus - 1.0
    diff_real = (far_real * factor).astype(jnp.bfloat16)
    diff_imag = (far_imag * factor).astype(jnp.bfloat16)
    conj_imag = -dft_imag
    back_half_real, back_half_imag = complex_matmul(dft_real, conj_imag, diff_real, diff_imag)
    back_half_real = back_half_real.astype(jnp.bfloat16)
    back_half_imag = back_half_imag.astype(jnp.bfloat16)
    back_real, back_imag = complex_matmul(back_half_real, back_half_imag, dft_real, conj_imag)
    object_real = probe_real * back_real + probe_imag * back_imag
    object_imag = probe_real * back_imag - probe_imag * back_real
    probe_grad_real = patch_real * back_real + patch_imag * back_imag
    probe_grad_imag = patch_real * back_imag - patch_imag * back_real
    energy = jnp.mean(patch_real * patch_real + patch_imag * patch_imag)
    return (
        jnp.stack([object_real, object_imag]),
        jnp.stack([probe_grad_real, probe_grad_imag]),
        energy,
    )


def tile_edges(values, offset):
    return shifted(values, "tile", offset)


def on_device(
    object_field,
    probe_field,
    amplitudes,
    pos_rows,
    pos_cols,
    counts,
    admm_dual,
    volume,
    proj_weights,
    ray_weights,
    angle_ids,
):
    half_side = PB // 2
    own_object = object_field[0]
    tile_cols = own_object.shape[2]
    from_left = tile_edges(own_object[:, :, tile_cols - half_side :], 1)
    from_right = tile_edges(own_object[:, :, :half_side], -1)
    extended = jnp.concatenate([from_left, own_object, from_right], axis=2)
    dft_real, dft_imag = dft_tables(PB)
    probe_real = probe_field[0]
    probe_imag = probe_field[1]
    zero_index = jnp.zeros((), jnp.int32)
    live_count = counts[0, 0]
    slot_total = amplitudes.shape[2]

    def slot_step(slot_index, state_tuple, weight):
        grad_sum, probe_sum, energy_sum = state_tuple
        anchor = (zero_index, pos_rows[0, 0, slot_index], pos_cols[0, 0, slot_index])
        object_patch = lax.dynamic_slice(extended, anchor, (2, PB, PB))
        object_part, probe_part, energy = patch_terms(
            object_patch[0],
            object_patch[1],
            probe_real,
            probe_imag,
            amplitudes[0, 0, slot_index],
            dft_real,
            dft_imag,
        )
        current = lax.dynamic_slice(grad_sum, anchor, (2, PB, PB))
        grad_sum = lax.dynamic_update_slice(grad_sum, current + weight * object_part, anchor)
        return (grad_sum, probe_sum + weight * probe_part, energy_sum + weight * energy)

    running = (
        jnp.zeros(extended.shape, jnp.float32),
        jnp.zeros((2, PB, PB), jnp.float32),
        jnp.zeros((), jnp.float32),
    )
    running = lax.fori_loop(
        0,
        slot_total,
        lambda slot_index, state_tuple: slot_step(
            slot_index, state_tuple, (slot_index < live_count).astype(jnp.float32)
        ),
        running,
    )
    grad_sum, probe_sum, energy_sum = running
    to_right_edge = tile_edges(grad_sum[:, :, :half_side], -1)
    to_left_edge = tile_edges(grad_sum[:, :, tile_cols + half_side :], 1)
    own_cells = grad_sum[:, :, half_side : half_side + tile_cols]
    own_cells = own_cells.at[:, :, :half_side].add(to_left_edge)
    own_cells = own_cells.at[:, :, tile_cols - half_side :].add(to_right_edge)
    probe_grad, energy = lax.psum((probe_sum, energy_sum), ("tile", "proj", "cuts"))
    new_probe = probe_field + probe_grad / (energy + 1e-05)
    probe_peak = jnp.max(probe_real * probe_real + probe_imag * probe_imag)
    new_object = (own_object + own_cells / (probe_peak + 1e-05))[None]
    slab_total = admm_dual.shape[1]
    first_row = (own_object.shape[1] - slab_total) // 2
    slab_values = new_object[:, 1, first_row : first_row + slab_total, :] + admm_dual
    arrived = lax.all_to_all(
        lax.all_to_all(slab_values, "proj", split_axis=2, concat_axis=0, tiled=True),
        "cuts",
        split_axis=1,
        concat_axis=0,
        tiled=True,
    )
    proj_count = lax.axis_size("proj")
    cuts_count = lax.axis_size("cuts")
    slab_dev = arrived.shape[1]
    u_share = arrived.shape[2]
    projections = proj_count * cuts_count
    arrived = arrived.reshape(cuts_count, proj_count, slab_dev, u_share).transpose(1, 0, 2, 3)
    target = (
        arrived.reshape(projections, slab_dev, u_share)
        .transpose(2, 0, 1)
        .reshape(u_share, projections * slab_dev)
    )
    angle_count = ray_weights.shape[0]
    x_share = volume.shape[1]
    width = volume.shape[2]
    onehot = (angle_ids[:, None] == jnp.arange(angle_count, dtype=jnp.int32)[None, :]).astype(
        jnp.float32
    )
    ray_table = jnp.dot(
        onehot, ray_weights, precision=lax.Precision.HIGHEST, preferred_element_type=jnp.float32
    )
    ray_sums = jnp.einsum("zxy,ay->azx", volume, ray_table, precision=lax.Precision.HIGHEST).astype(
        jnp.bfloat16
    )
    spread = onehot.astype(jnp.bfloat16)[:, :, None, None] * ray_sums[:, None, :, :]
    spread = spread.transpose(1, 3, 0, 2).reshape(angle_count * x_share, projections * slab_dev)
    weight_flat = proj_weights.reshape(angle_count * x_share, width)
    partial_term = lax.dot_general(
        weight_flat, spread, (((0,), (0,)), ((), ())), preferred_element_type=jnp.float32
    )
    row_start = lax.axis_index(("tile", "proj")) * u_share
    own_rows = lax.dynamic_slice_in_dim(partial_term, row_start, u_share, 0)
    partial_term = lax.dynamic_update_slice_in_dim(partial_term, own_rows - target, row_start, 0)
    summed = lax.psum(partial_term, ("tile", "proj"))
    residue = summed.astype(jnp.bfloat16)
    backproj = matmul(weight_flat, residue)
    backproj = backproj.reshape(angle_count, x_share, projections, slab_dev)
    back_sums = jnp.einsum("gxaz,ag->azx", backproj, onehot, precision=lax.Precision.HIGHEST)
    gradient = jnp.einsum("azx,ay->zxy", back_sums, ray_table, precision=lax.Precision.HIGHEST)
    new_volume = volume - tomo_step * gradient
    return (new_object, new_probe, new_volume)


def solution(mesh):
    in_specs = (
        P(("proj", "cuts"), None, None, "tile"),
        P(),
        P(("proj", "cuts"), "tile", None, None, None),
        P(("proj", "cuts"), "tile", None),
        P(("proj", "cuts"), "tile", None),
        P(("proj", "cuts"), "tile"),
        P(("proj", "cuts"), None, "tile"),
        P("cuts", ("tile", "proj"), None),
        P(None, ("tile", "proj"), None),
        P(),
        P(),
    )
    out_specs = (P(("proj", "cuts"), None, None, "tile"), P(), P("cuts", ("tile", "proj"), None))
    return jax.shard_map(
        on_device, mesh=mesh, in_specs=in_specs, out_specs=out_specs, check_vma=False
    )
```

profile of v0, /device:TPU:64, one launch (start us, length us, event | category | flops | bytes accessed | tf_op | source)
XLA Modules:
  0.0 1082.3 jit_solution(16087223290670484655)
XLA Ops:
  7.2 3.2 copy.38
  13.8 5.3 collective-permute-start
  20.4 3.4 fusion.127
  25.5 4.1 mul.437
  30.3 3.0 pad_maximum_fusion
  34.9 254.5 %while.23 = (s32[]{:T(128)}, f32[2,384,768]{1,2,0:T(8,128)}, f32[2,256,256]{2,1,0:T(8,128)}, f32[]{:T(128)}, s32[1,1,6]{2,1,0:T(1,128)S(1)}, /*index=5*/s32[1,1,...) while((s32[]{:T(128)}, f32[2,384,768]{1,2,0:T(8,128)}, ...), condition=%wide.region_2.3_spmd.clone.clone, body=%wide.region_0.2_spmd.clone.clone.sunk | while | flops 558956544 | bytes 22151564 | solution.py:118
  64.0 2.2 fusion.233
  68.2 6.5 dynamic_update_slice.17
  106.3 2.2 fusion.233
  110.5 6.5 dynamic_update_slice.17
  148.8 2.2 fusion.233
  153.0 6.1 dynamic_update_slice.17
  180.6 2.1 multiply_convert_fusion.39
  190.8 2.2 fusion.233
  195.0 6.6 dynamic_update_slice.17
  233.3 2.2 fusion.233
  237.5 6.5 dynamic_update_slice.17
  275.8 2.2 fusion.233
  280.0 6.5 dynamic_update_slice.17
  291.5 2.8 collective-permute-start.2
  295.6 4.3 fusion.138
  301.4 2.7 slice.97
  313.8 9.8 all-to-all-start
  323.7 79.2 %psum.22 = f32[]{:T(128)} all-reduce(f32[]{:T(128)} %get-tuple-element.384), channel_id=1, replica_groups=mesh['tile'=4,'proj'=16,'cuts'=4] {'tile','proj','cuts'}, use_global_device_ids=true, to_apply=%region_5.6 | all-reduce | flops 1 | bytes 8 | tf_op jit(solution)/shard_map/psum | solution.py:132
  405.8 6.0 all-to-all-start.1
  411.8 145.5 %all-reduce.3.cloned.1.call-done = f32[2,256,256]{2,1,0:T(8,128)} async-done(((f32[2,256,256]{2,1,0:T(8,128)}), f32[2,256,256]{2,1,0:T(8,128)}) %all-reduce.3.cloned.1.call-update) | async-done | bytes 524304 | tf_op jit(solution)/shard_map/psum | solution.py:132
  559.2 3.0 copy.48
  566.2 495.1 %all-reduce.4 = bf16[2048,512]{0,1:T(8,128)(2,1)} all-reduce(f32[2048,512]{0,1:T(8,128)} %dynamic_update_slice.13), channel_id=1, replica_groups=mesh['tile'=4,'proj'=16,'cuts'=4] {'tile','proj'}, use_global_device_ids=true, to_apply=%region_6.7 | all-reduce | flops 1048576 | bytes 6291456 | tf_op jit(solution)/shard_map/psum | solution.py:178
  1061.4 2.9 fusion.124
  1064.2 2.5 reshape.122
  1066.7 3.8 fusion.130
  1070.7 4.7 convolution_subtract_fusion.4
  (227 shorter events, 199.5 us)
Async XLA Ops:
  7.2 288.4 %copy-start = (bf16[16,32,2048]{2,1,0:T(8,128)(2,1)S(1)}, bf16[16,32,2048]{2,1,0:T(8,128)(2,1)}, u32[]{:S(2)}) copy-start(bf16[16,32,2048]{2,1,0:T(8,128)(2,1)} %param.25) | copy-start | bytes 6291460
  7.2 11.9 %copy-start.12 = (s32[64]{0:T(128)S(1)}, s32[64]{0:T(128)}, u32[]{:S(2)}) copy-start(s32[64]{0:T(128)} %param.27) | copy-start | bytes 772
  7.2 11.9 %copy-start.8 = (f32[16,2048]{1,0:T(8,128)S(1)}, f32[16,2048]{1,0:T(8,128)}, u32[]{:S(2)}) copy-start(f32[16,2048]{1,0:T(8,128)} %param.26) | copy-start | bytes 393220
  7.2 550.1 %all-reduce.3.cloned.1.call-start = ((), (), s32[]{:S(2)}) async-start(), calls=%async_computation.2 | async-start | bytes 1048576 | tf_op jit(solution)/shard_map/psum | solution.py:132
  12.5 17.9 %collective-permute-start.1 = (f32[2,384,128]{1,2,0:T(8,128)}, f32[2,384,128]{1,2,0:T(8,128)S(1)}, u32[]{:S(2)}, u32[]{:S(2)}) collective-permute-start(f32[2,384,128]{1,2,0:T(8,128)} %get-tuple-element.557), channel_id=1, source_target_pairs={{64,0},{128,64},{192,128},{65,1},{129,65},{193,129},{66,2},{130,66... | collective-permute-start | bytes 1179656 | tf_op jit(solution)/shard_map/ppermute | solution.py:14
  13.8 16.6 %collective-permute-start = (f32[2,384,128]{1,2,0:T(8,128)}, f32[2,384,128]{1,2,0:T(8,128)}, u32[]{:S(2)}, u32[]{:S(2)}) collective-permute-start(f32[2,384,128]{1,2,0:T(8,128)} %get-tuple-element.556), channel_id=1, source_target_pairs={{0,64},{64,128},{128,192},{1,65},{65,129},{129,193},{2,66},{66,130... | collective-permute-start | bytes 1179656 | tf_op jit(solution)/shard_map/ppermute | solution.py:14
  19.6 0.8 copy-start.6
  23.9 5.7 copy-start.4
  33.4 1.6 copy-start.10
  33.4 1.6 copy-start.11
  60.5 3.5 copy-start.1
  102.8 3.4 copy-start.1
  145.3 3.5 copy-start.1
  187.4 3.5 copy-start.1
  229.9 3.4 copy-start.1
  272.4 3.4 copy-start.1
  291.5 12.6 %collective-permute-start.2 = (f32[2,384,128]{1,2,0:T(8,128)}, f32[2,384,128]{1,2,0:T(8,128)}, u32[]{:S(2)}, u32[]{:S(2)}) collective-permute-start(f32[2,384,128]{1,2,0:T(8,128)} %get-tuple-element.555), channel_id=1, source_target_pairs={{0,64},{64,128},{128,192},{1,65},{65,129},{129,193},{2,66},{66,130... | collective-permute-start | bytes 1179656 | tf_op jit(solution)/shard_map/ppermute | solution.py:14
  294.3 11.9 %collective-permute-start.3 = (f32[2,384,128]{1,2,0:T(8,128)S(1)}, f32[2,384,128]{1,2,0:T(8,128)}, u32[]{:S(2)}, u32[]{:S(2)}) collective-permute-start(f32[2,384,128]{1,2,0:T(8,128)S(1)} %get-tuple-element.554), channel_id=1, source_target_pairs={{64,0},{128,64},{192,128},{65,1},{129,65},{193,129},{66,2},{130,66... | collective-permute-start | bytes 1179656 | tf_op jit(solution)/shard_map/ppermute | solution.py:14
  295.6 4.3 copy-start.9
  295.6 4.5 copy-start.5
  304.0 4.0 copy-start.2
  309.7 1.1 copy-start.3
  313.8 89.7 %all-to-all-start = ((f32[16,1,1024]{2,1,0:T(1,128)}), f32[16,1,1024]{2,1,0:T(1,128)S(1)}, u32[]{:S(2)}, u32[]{:S(2)}) async-start(f32[16,1,1024]{2,1,0:T(1,128)} %reshape.128), calls=%async_computation | async-start | bytes 131072 | tf_op jit(solution)/shard_map/all_to_all | solution.py:140
  405.8 156.4 %all-to-all-start.1 = ((f32[4,1,4096]{2,1,0:T(1,128)}), f32[4,1,4096]{2,1,0:T(1,128)S(1)}, u32[]{:S(2)}, u32[]{:S(2)}) async-start(f32[4,1,4096]{2,1,0:T(1,128)} %reshape.130), calls=%async_computation.1 | async-start | bytes 131072 | tf_op jit(solution)/shard_map/all_to_all | solution.py:139
  1066.7 4.0 copy-start.7
Sparse Core Ops, SparseCore 0:
  304.2 253.0 all-reduce.2
where the time goes:
time: 1090 us; the launch traced here: 1080 us
  blocking collectives  574 us (53%)
  waiting for transfers between devices  146 us (13%)
  matrix products  141 us (13%)
  local copies, waits for them, and re-layouts  101 us (9%)
  other arithmetic  45.9 us (4%)
  loops' own time  31.6 us (3%)
  starting transfers between devices  26.6 us (2%)
  between operations  15.6 us (1%)
    psum x1, blocking collectives, on_device(): summed = lax.psum(partial_term, ('tile', 'proj'))  495 us
    psum x1, waiting for transfers between devices, on_device(): lax.psum((probe_sum, energy_sum), ('tile', 'proj', 'cuts'))  145 us
    dot_general x97, matrix products, matmul(): return jnp.dot(left, right, preferred_element_type=jnp.float32)  125 us
    psum x1, blocking collectives, on_device(): lax.psum((probe_sum, energy_sum), ('tile', 'proj', 'cuts'))  79.2 us
    dynamic_update_slice x12, local copies, waits for them, and re-layouts, slot_step(): lax.dynamic_update_slice(grad_sum, current + weight * object_part, anchor)  39.9 us
    another operation x1, loops' own time, on_device(): lax.fori_loop(0, slot_total, lambda slot_index, state_tuple: slot_step(sl...  31.6 us
  transfers between devices with their start and end apart: 7, of which 2 were waited for; matrix products, arithmetic and copies ran while one was open for 3% of the time, Pallas kernels for 0%

commit v1 on v0

--- a/solution.py
+++ b/solution.py
@@ -1,11 +1,22 @@
+import functools
 import math
 import jax
 import jax.numpy as jnp
 from jax import lax
 from jax.sharding import PartitionSpec as P
+from jax.lax import psum
 
 PB = 256
 tomo_step = 1.0
+
+
+def wrap_plate(arr_in, across, mesh_dim):
+    for k in (across, mesh_dim):
+        arr_in = psum(arr_in, k)
+    return arr_in
+
+
+find_point = functools.partial(wrap_plate, across=("proj", "cuts"), mesh_dim="tile")
 
 
 def shifted(value, axis, steps):
@@ -129,7 +140,7 @@
     own_cells = grad_sum[:, :, half_side : half_side + tile_cols]
     own_cells = own_cells.at[:, :, :half_side].add(to_left_edge)
     own_cells = own_cells.at[:, :, tile_cols - half_side :].add(to_right_edge)
-    probe_grad, energy = lax.psum((probe_sum, energy_sum), ("tile", "proj", "cuts"))
+    probe_grad, energy = find_point((probe_sum, energy_sum))
     new_probe = probe_field + probe_grad / (energy + 1e-05)
     probe_peak = jnp.max(probe_real * probe_real + probe_imag * probe_imag)
     new_object = (own_object + own_cells / (probe_peak + 1e-05))[None]

time: 1090 us -> 1020 us (0.936)
  waiting for transfers between devices: 146 us -> 41.8 us
  blocking collectives: 574 us -> 605 us
    psum x1 -> x2, waiting for transfers between devices: 145 us -> 33 us  [wrap_plate(): arr_in = psum(arr_in, k)]
    psum x1 -> x2, blocking collectives: 79.2 us -> 136 us  [wrap_plate(): arr_in = psum(arr_in, k)]
    psum x1, blocking collectives: 495 us -> 469 us  [on_device(): summed = lax.psum(partial_term, ('tile', 'proj'))]
  transfers between devices with their start and end apart: 7 -> 8, of which waited for: 2 -> 4; matrix products, arithmetic and copies ran while one was open for 3% -> 4% of each run, Pallas kernels for 0% -> 0%
where the time goes in v1:
time: 1020 us; the launch traced here: 1010 us
  blocking collectives  605 us (59%)
  matrix products  141 us (14%)
  local copies, waits for them, and re-layouts  106 us (10%)
  other arithmetic  44.5 us (4%)
  waiting for transfers between devices  41.8 us (4%)
  loops' own time  30.6 us (3%)
  starting transfers between devices  27.8 us (3%)
  between operations  15.6 us (2%)
    psum x1, blocking collectives, on_device(): summed = lax.psum(partial_term, ('tile', 'proj'))  469 us
    psum x2, blocking collectives, wrap_plate(): arr_in = psum(arr_in, k)  136 us
    dot_general x97, matrix products, matmul(): return jnp.dot(left, right, preferred_element_type=jnp.float32)  126 us
    dynamic_update_slice x12, local copies, waits for them, and re-layouts, slot_step(): lax.dynamic_update_slice(grad_sum, current + weight * object_part, anchor)  39.9 us
    psum x2, waiting for transfers between devices, wrap_plate(): arr_in = psum(arr_in, k)  33 us
    another operation x1, loops' own time, on_device(): lax.fori_loop(0, slot_total, lambda slot_index, state_tuple: slot_step(sl...  30.6 us
  transfers between devices with their start and end apart: 8, of which 4 were waited for; matrix products, arithmetic and copies ran while one was open for 4% of the time, Pallas kernels for 0%

profile of v1, /device:TPU:64, one launch (start us, length us, event | category | flops | bytes accessed | tf_op | source)
XLA Modules:
  0.0 1011.9 jit_solution(4508090164317795506)
XLA Ops:
  7.2 3.2 copy.38
  13.8 5.3 collective-permute-start
  20.4 3.4 fusion.127
  26.8 3.0 pad_maximum_fusion
  31.4 257.5 %while.23 = (s32[]{:T(128)}, f32[2,384,768]{1,2,0:T(8,128)}, f32[2,256,256]{2,1,0:T(8,128)}, f32[]{:T(128)}, s32[1,1,6]{2,1,0:T(1,128)}, /*index=5*/s32[1,1,6]{2...) while((s32[]{:T(128)}, f32[2,384,768]{1,2,0:T(8,128)}, ...), condition=%wide.region_2.3_spmd.clone.clone, body=%wide.region_0.2_spmd.clone.clone.sunk | while | flops 558956544 | bytes 22151564 | solution.py:129
  60.9 2.2 fusion.233
  65.1 6.5 dynamic_update_slice.17
  103.7 2.2 fusion.233
  107.9 6.5 dynamic_update_slice.17
  146.7 2.2 fusion.233
  150.9 6.1 dynamic_update_slice.17
  189.3 2.2 fusion.233
  193.5 6.5 dynamic_update_slice.17
  232.3 2.2 fusion.233
  236.5 6.5 dynamic_update_slice.17
  275.2 2.2 fusion.233
  279.4 6.5 dynamic_update_slice.17
  291.0 4.4 collective-permute-start.2
  298.4 3.4 mul.437
  314.0 9.9 all-to-all-start
  324.0 3.2 fusion.138
  327.2 6.8 all-to-all-done
  336.2 5.2 all-to-all-start.1
  341.5 123.2 %psum.37 = f32[]{:T(128)} all-reduce(f32[]{:T(128)} %get-tuple-element.384), channel_id=1, replica_groups=mesh['tile'=4,'proj'=16,'cuts'=4] {'proj','cuts'}, use_global_device_ids=true, to_apply=%region_6.7 | all-reduce | flops 1 | bytes 8 | tf_op jit(solution)/shard_map/psum | solution.py:15
  464.7 12.3 %psum.38 = f32[]{:T(128)} all-reduce(f32[]{:T(128)} %psum.37), channel_id=1, replica_groups=mesh['tile'=4,'proj'=16,'cuts'=4] {'tile'}, use_global_device_ids=true, to_apply=%region_7.8 | all-reduce | flops 1 | bytes 8 | tf_op jit(solution)/shard_map/psum | solution.py:15
  477.7 33.0 %all-reduce.4.cloned.1.call-done = f32[2,256,256]{2,1,0:T(8,128)} async-done(((f32[2,256,256]{2,1,0:T(8,128)}), f32[2,256,256]{2,1,0:T(8,128)}) %all-reduce.4.cloned.1.call-update) | async-done | bytes 524304 | tf_op jit(solution)/shard_map/psum | solution.py:15
  510.7 3.0 copy.48
  517.7 469.1 %all-reduce.7 = bf16[2048,512]{0,1:T(8,128)(2,1)} all-reduce(f32[2048,512]{0,1:T(8,128)} %dynamic_update_slice.13), channel_id=1, replica_groups=mesh['tile'=4,'proj'=16,'cuts'=4] {'tile','proj'}, use_global_device_ids=true, to_apply=%region_8.9 | all-reduce | flops 1048576 | bytes 6291456 | tf_op jit(solution)/shard_map/psum | solution.py:189
  986.8 3.9 fusion.124
  990.7 3.8 reshape.122
  994.5 3.8 fusion.130
  998.4 4.7 convolution_subtract_fusion.4
  (227 shorter events, 208.8 us)
Async XLA Ops:
  7.2 316.8 %copy-start = (bf16[16,32,2048]{2,1,0:T(8,128)(2,1)S(1)}, bf16[16,32,2048]{2,1,0:T(8,128)(2,1)}, u32[]{:S(2)}) copy-start(bf16[16,32,2048]{2,1,0:T(8,128)(2,1)} %param.25) | copy-start | bytes 6291460
  7.2 12.0 %copy-start.8 = (f32[16,2048]{1,0:T(8,128)S(1)}, f32[16,2048]{1,0:T(8,128)}, u32[]{:S(2)}) copy-start(f32[16,2048]{1,0:T(8,128)} %param.26) | copy-start | bytes 393220
  7.2 12.0 %copy-start.9 = (s32[64]{0:T(128)S(1)}, s32[64]{0:T(128)}, u32[]{:S(2)}) copy-start(s32[64]{0:T(128)} %param.27) | copy-start | bytes 772
  12.4 11.6 %copy-start.4 = (f32[2,256,256]{2,1,0:T(8,128)S(1)}, f32[2,256,256]{2,1,0:T(8,128)}, u32[]{:S(2)}) copy-start(f32[2,256,256]{2,1,0:T(8,128)} %param.18) | copy-start | bytes 1572868
  12.4 13.1 %collective-permute-start.1 = (f32[2,384,128]{1,2,0:T(8,128)}, f32[2,384,128]{1,2,0:T(8,128)S(1)}, u32[]{:S(2)}, u32[]{:S(2)}) collective-permute-start(f32[2,384,128]{1,2,0:T(8,128)} %get-tuple-element.557), channel_id=1, source_target_pairs={{64,0},{128,64},{192,128},{65,1},{129,65},{193,129},{66,2},{130,66... | collective-permute-start | bytes 1179656 | tf_op jit(solution)/shard_map/ppermute | solution.py:25
  13.8 12.9 %collective-permute-start = (f32[2,384,128]{1,2,0:T(8,128)}, f32[2,384,128]{1,2,0:T(8,128)}, u32[]{:S(2)}, u32[]{:S(2)}) collective-permute-start(f32[2,384,128]{1,2,0:T(8,128)} %get-tuple-element.556), channel_id=1, source_target_pairs={{0,64},{64,128},{128,192},{1,65},{65,129},{129,193},{2,66},{66,130... | collective-permute-start | bytes 1179656 | tf_op jit(solution)/shard_map/ppermute | solution.py:25
  19.6 0.8 copy-start.6
  57.5 3.4 copy-start.1
  100.3 3.5 copy-start.1
  143.3 3.4 copy-start.1
  185.8 3.5 copy-start.1
  228.8 3.4 copy-start.1
  271.8 3.5 copy-start.1
  291.0 14.8 %collective-permute-start.2 = (f32[2,384,128]{1,2,0:T(8,128)}, f32[2,384,128]{1,2,0:T(8,128)}, u32[]{:S(2)}, u32[]{:S(2)}) collective-permute-start(f32[2,384,128]{1,2,0:T(8,128)} %get-tuple-element.555), channel_id=1, source_target_pairs={{0,64},{64,128},{128,192},{1,65},{65,129},{129,193},{2,66},{66,130... | collective-permute-start | bytes 1179656 | tf_op jit(solution)/shard_map/ppermute | solution.py:25
  295.4 7.4 copy-start.5
  295.4 11.5 %collective-permute-start.3 = (f32[2,384,128]{1,2,0:T(8,128)}, f32[2,384,128]{1,2,0:T(8,128)}, u32[]{:S(2)}, u32[]{:S(2)}) collective-permute-start(f32[2,384,128]{1,2,0:T(8,128)} %get-tuple-element.554), channel_id=1, source_target_pairs={{64,0},{128,64},{192,128},{65,1},{129,65},{193,129},{66,2},{130,66... | collective-permute-start | bytes 1179656 | tf_op jit(solution)/shard_map/ppermute | solution.py:25
  304.1 3.9 copy-start.2
  308.2 1.1 copy-start.3
  314.0 20.0 %all-to-all-start = ((f32[16,1,1024]{2,1,0:T(1,128)}), f32[16,1,1024]{2,1,0:T(1,128)S(1)}, u32[]{:S(2)}, u32[]{:S(2)}) async-start(f32[16,1,1024]{2,1,0:T(1,128)} %reshape.128), calls=%async_computation | async-start | bytes 131072 | tf_op jit(solution)/shard_map/all_to_all | solution.py:151
  323.9 186.7 %all-reduce.4.cloned.1.call-start = ((), (), s32[]{:S(2)}) async-start(), calls=%async_computation.2 | async-start | bytes 1048576 | tf_op jit(solution)/shard_map/psum | solution.py:15
  327.2 14.2 %copy-start.10 = (s32[64]{0:T(128)S(1)}, s32[64]{0:T(128)}, u32[]{:S(2)}) copy-start(s32[64]{0:T(128)} %param.27) | copy-start | bytes 772
  336.2 177.5 %all-to-all-start.1 = ((f32[4,1,4096]{2,1,0:T(1,128)}), f32[4,1,4096]{2,1,0:T(1,128)S(1)}, u32[]{:S(2)}, u32[]{:S(2)}) async-start(f32[4,1,4096]{2,1,0:T(1,128)} %reshape.130), calls=%async_computation.1 | async-start | bytes 131072 | tf_op jit(solution)/shard_map/all_to_all | solution.py:150
  341.4 661.7 %all-reduce.6.cloned.1.call-start = ((), (), s32[]{:S(2)}) async-start(), calls=%async_computation.3 | async-start | bytes 1048576 | tf_op jit(solution)/shard_map/psum | solution.py:15
  994.5 4.0 copy-start.7
Sparse Core Ops, SparseCore 0:
  328.8 181.7 all-reduce.3
  513.0 50.4 all-reduce.5
